TPU v7x, 256 devices: a whole 4x4x8 slice. The times are simulated.
256 devices in a mesh: cluster: 8 (over z), sub: 32 (over x, y, core).
Axes of the slice: x: 4, y: 4, z: 8, core: 2. Of those that a mesh axis runs over, the one named last changes fastest.
Arguments:
- dual_ops: bfloat16 [8, 32, 2048, 2048], P('cluster', 'sub'), as said below
- corner_coupling: float32 [8, 32, 48, 2048], P('cluster', 'sub'), may hold values from -0.3 to 0.3
- coarse_inverse: float32 [32, 128, 128], P('sub'), as said below
- corner_map: int32 [8, 32, 48], P('cluster', 'sub'), may hold values from 0 to 127, as said below
- interface_tiles: int32 [8, 32, 4], P('cluster', 'sub'), may hold values from 1 to 4, as said below
- gap_terms: float32 [8, 32, 2048, 128], P('cluster', 'sub')
Outputs:
- multipliers: float32 [8, 32, 2048, 128], P('cluster', 'sub')
- residual: float32 [8, 32, 2048, 128], P('cluster', 'sub')
Inputs may be any that keep to these rules, and one draw needn't show every extreme that they name: interface_tiles[c, s, k] counts the tiles that subdomain (c, s) shares with the subdomain at sub distance -2, -1, +1, +2 for k = 0..3, wrapping around 32; the count for distance +d equals that neighbour's count for distance -d; in every c some subdomain has 4 for all four. `corner_map`: the 48 entries of one subdomain are distinct. `dual_ops`: each matrix is symmetric positive definite. `coarse_inverse`: each matrix is symmetric positive definite.
All inputs are finite; a program needn't handle non-finite values.
Results may differ from a plain program's by a relative error of at most 0.009.
Values sent between devices are 32-bit elements; how exact they have to be, the bound alone decides.
No kernel may reach another device: no remote copies, remote signals or barrier semaphores. Data moves between devices by JAX's collectives and lax.ppermute only.
A program may use at most 64 MiB of HBM per device.

v0:
```python
import jax
import jax.numpy as jnp
from jax import lax
from jax.sharding import PartitionSpec as P

TILE = 128
MAXT = 4
NCOARSE = 128
ITERS = 3


def passed_along(block, axis, distance):
    devices = range(lax.axis_size(axis))
    route = [((i - distance) % len(devices), i) for i in devices]
    return lax.ppermute(block, axis, route)


def extract_run(values_in, start_row, row_count):
    run_rows = MAXT * TILE
    run_block = lax.dynamic_slice_in_dim(values_in, start_row, run_rows, 0)
    keep_mask = jnp.arange(run_rows, dtype=jnp.int32)[:, None] < row_count
    return jnp.where(keep_mask, run_block, jnp.zeros_like(run_block))


def insert_run(run_block, start_row, dual_rows):
    padded = jnp.zeros((dual_rows + run_block.shape[0], run_block.shape[1]), run_block.dtype)
    return lax.dynamic_update_slice_in_dim(padded, run_block, start_row, 0)[:dual_rows]


def local(dual_ops, corner_coupling, coarse_inverse, corner_map, interface_tiles, gap_terms):
    highest = lax.Precision.HIGHEST
    operator = dual_ops[0, 0]
    coupling = corner_coupling[0, 0]
    inverse = coarse_inverse[0]
    corners = corner_map[0, 0]
    lengths = interface_tiles[0, 0] * TILE
    run_start = jnp.concatenate([jnp.zeros((1,), jnp.int32), jnp.cumsum(lengths)[:3]])
    dual_rows = operator.shape[0]
    live_mask = jnp.arange(dual_rows, dtype=jnp.int32)[:, None] < jnp.sum(lengths)
    onehot = (corners[:, None] == jnp.arange(NCOARSE, dtype=jnp.int32)[None, :]).astype(jnp.float32)

    def assemble(values_in):
        incoming = [None, None, None, None]
        for run_index, distance in enumerate((-2, -1, 1, 2)):
            outgoing = extract_run(values_in, run_start[3 - run_index], lengths[3 - run_index])
            incoming[run_index] = passed_along(outgoing, "sub", -distance)
        assembled = jnp.where(live_mask, values_in, jnp.zeros_like(values_in))
        for run_index in range(4):
            assembled = assembled + insert_run(incoming[run_index], run_start[run_index], dual_rows)
        return assembled

    residual = assemble(gap_terms[0, 0])
    direction = residual
    multipliers = jnp.zeros_like(residual)
    norm_now = lax.psum(jnp.sum(residual * residual, axis=0), ("cluster", "sub"))
    for iteration in range(ITERS):
        local_part = jnp.dot(
            operator, direction.astype(jnp.bfloat16), preferred_element_type=jnp.float32
        )
        corner_values = jnp.dot(coupling, direction, precision=highest)
        coarse_part = jnp.dot(onehot.T, corner_values, precision=highest)
        coarse_total = lax.psum(coarse_part, "cluster")
        coarse_solution = jnp.dot(inverse, coarse_total, precision=highest)
        corner_back = jnp.dot(onehot, coarse_solution, precision=highest)
        image = assemble(local_part + jnp.dot(coupling.T, corner_back, precision=highest))
        curvature = lax.psum(jnp.sum(direction * image, axis=0), ("cluster", "sub"))
        step_size = norm_now / curvature
        multipliers = multipliers + step_size * direction
        residual = residual - step_size * image
        norm_next = lax.psum(jnp.sum(residual * residual, axis=0), ("cluster", "sub"))
        direction = residual + norm_next / norm_now * direction
        norm_now = norm_next
    return (multipliers[None, None], residual[None, None])


def solution(mesh):
    in_specs = (
        P("cluster", "sub", None, None),
        P("cluster", "sub", None, None),
        P("sub", None, None),
        P("cluster", "sub", None),
        P("cluster", "sub", None),
        P("cluster", "sub", None, None),
    )
    out_specs = (P("cluster", "sub", None, None), P("cluster", "sub", None, None))
    return jax.shard_map(local, mesh=mesh, in_specs=in_specs, out_specs=out_specs, check_vma=False)
```

profile of v0, /device:TPU:1, one launch (start us, length us, event | category | flops | bytes accessed | tf_op | source)
XLA Modules:
  0.0 746.1 jit_solution(15423645180526299071)
XLA Ops:
  18.1 2.8 collective-permute-start.1
  22.6 4.8 collective-permute-start.3
  46.0 70.0 %all-reduce.9.cloned.1.call-done = f32[128,128]{1,0:T(8,128)} async-done(((f32[128,128]{1,0:T(8,128)}), f32[128,128]{1,0:T(8,128)}) %all-reduce.9.cloned.1.call-update) | async-done | bytes 65552 | tf_op jit(solution)/shard_map/psum | solution.py:62
  118.4 6.3 fusion.6
  125.8 6.7 collective-permute-start.5
  132.6 4.1 collective-permute-start.7
  147.2 2.8 multiply_reduce_fusion.4
  150.0 78.7 %all-reduce.4 = (f32[128]{0:T(128)S(1)}, f32[128]{0:T(128)S(1)}) all-reduce(f32[128]{0:T(128)} %get-tuple-element.5, f32[128]{0:T(128)} %get-tuple-element.4), channel_id=1, replica_groups=mesh['cluster'=8,'sub'=32] {'cluster','sub'}, use_global_device_ids=true, to_apply=%region_3.4 | all-reduce | flops 256 | bytes 2048 | tf_op jit(solution)/shard_map/psum | solution.py:55
  229.6 72.4 %psum.66 = f32[128]{0:T(128)S(1)} all-reduce(f32[128]{0:T(128)S(1)} %multiply_reduce_fusion.3), channel_id=1, replica_groups=mesh['cluster'=8,'sub'=32] {'cluster','sub'}, use_global_device_ids=true, to_apply=%region_8.9 | all-reduce | flops 128 | bytes 1024 | tf_op jit(solution)/shard_map/psum | solution.py:70
  305.5 7.2 fusion.2
  312.7 56.5 %all-reduce.11.cloned.1.call-done = f32[128,128]{1,0:T(8,128)} async-done(((f32[128,128]{1,0:T(8,128)}), f32[128,128]{1,0:T(8,128)}) %all-reduce.11.cloned.1.call-update) | async-done | bytes 65552 | tf_op jit(solution)/shard_map/psum | solution.py:62
  374.1 6.7 collective-permute-start.9
  381.5 3.6 collective-permute-start.11
  395.8 4.2 multiply_reduce_fusion.2
  400.0 78.7 %psum.68 = f32[128]{0:T(128)} all-reduce(f32[128]{0:T(128)} %get-tuple-element.12), channel_id=1, replica_groups=mesh['cluster'=8,'sub'=32] {'cluster','sub'}, use_global_device_ids=true, to_apply=%region_11.12 | all-reduce | flops 128 | bytes 1024 | tf_op jit(solution)/shard_map/psum | solution.py:66
  479.3 3.0 multiply_reduce_fusion.1
  482.3 72.5 %psum.69 = f32[128]{0:T(128)S(1)} all-reduce(f32[128]{0:T(128)} %get-tuple-element.10), channel_id=1, replica_groups=mesh['cluster'=8,'sub'=32] {'cluster','sub'}, use_global_device_ids=true, to_apply=%region_13.14 | all-reduce | flops 128 | bytes 1024 | tf_op jit(solution)/shard_map/psum | solution.py:70
  558.7 7.2 fusion
  565.9 56.7 %all-reduce.13.cloned.1.call-done = f32[128,128]{1,0:T(8,128)} async-done(((f32[128,128]{1,0:T(8,128)}), f32[128,128]{1,0:T(8,128)}) %all-reduce.13.cloned.1.call-update) | async-done | bytes 65552 | tf_op jit(solution)/shard_map/psum | solution.py:62
  627.4 6.7 collective-permute-start.13
  634.9 3.6 collective-permute-start.15
  649.1 3.7 multiply_reduce_fusion
  652.8 78.6 %psum.71 = f32[128]{0:T(128)} all-reduce(f32[128]{0:T(128)S(1)} %get-tuple-element.8), channel_id=1, replica_groups=mesh['cluster'=8,'sub'=32] {'cluster','sub'}, use_global_device_ids=true, to_apply=%region_16.17 | all-reduce | flops 128 | bytes 1024 | tf_op jit(solution)/shard_map/psum | solution.py:66
  732.1 3.3 subtract_bitcast_fusion
  (145 shorter events, 81.6 us)
Async XLA Ops:
  7.2 36.8 %copy-start = (f32[1,1,48,2048]{3,2,1,0:T(8,128)S(1)}, f32[1,1,48,2048]{3,2,1,0:T(8,128)}, u32[]{:S(2)}) copy-start(f32[1,1,48,2048]{3,2,1,0:T(8,128)} %param.7) | copy-start | bytes 1179652
  7.2 108.8 %all-reduce.9.cloned.1.call-start = ((), (), s32[]{:S(2)}) async-start(), calls=%async_computation | async-start | bytes 131072 | tf_op jit(solution)/shard_map/psum | solution.py:62
  18.1 14.6 %collective-permute-start.1 = (f32[512,128]{0,1:T(8,128)S(1)}, f32[512,128]{0,1:T(8,128)S(1)}, u32[]{:S(2)}, u32[]{:S(2)}) collective-permute-start(f32[512,128]{0,1:T(8,128)S(1)} %bitcast_select_fusion.2), channel_id=1, source_target_pairs={{31,0},{0,1},{1,2},{2,3},{3,4},{4,5},{5,6},{6,7},{7,8},{8,9},{9,10... | collective-permute-start | bytes 786440 | tf_op jit(solution)/shard_map/ppermute | solution.py:15
  21.0 14.7 %collective-permute-start.2 = (f32[512,128]{0,1:T(8,128)S(1)}, f32[512,128]{0,1:T(8,128)}, u32[]{:S(2)}, u32[]{:S(2)}) collective-permute-start(f32[512,128]{0,1:T(8,128)S(1)} %bitcast_select_fusion.1), channel_id=1, source_target_pairs={{1,0},{2,1},{3,2},{4,3},{5,4},{6,5},{7,6},{8,7},{9,8},{10,9},{11,1... | collective-permute-start | bytes 786440 | tf_op jit(solution)/shard_map/ppermute | solution.py:15
  22.6 9.4 %copy-start.7 = (pred[512]{0:T(512)(128)(4,1)}, pred[512]{0:T(512)(128)(4,1)S(1)}, u32[]{:S(2)}) copy-start(pred[512]{0:T(512)(128)(4,1)S(1)} %iota_compare_fusion.5) | copy-start | bytes 1540
  22.6 16.2 %collective-permute-start.3 = (f32[512,128]{0,1:T(8,128)S(1)}, f32[512,128]{0,1:T(8,128)S(1)}, u32[]{:S(2)}, u32[]{:S(2)}) collective-permute-start(f32[512,128]{0,1:T(8,128)S(1)} %fusion.38), channel_id=1, source_target_pairs={{2,0},{3,1},{4,2},{5,3},{6,4},{7,5},{8,6},{9,7},{10,8},{11,9},{12,... | collective-permute-start | bytes 786440 | tf_op jit(solution)/shard_map/ppermute | solution.py:15
  28.2 13.6 %collective-permute-start = (f32[512,128]{0,1:T(8,128)S(1)}, f32[512,128]{0,1:T(8,128)S(1)}, u32[]{:S(2)}, u32[]{:S(2)}) collective-permute-start(f32[512,128]{0,1:T(8,128)S(1)} %bitcast_select_fusion.3), channel_id=1, source_target_pairs={{30,0},{31,1},{0,2},{1,3},{2,4},{3,5},{4,6},{5,7},{6,8},{7,9},{8,1... | collective-permute-start | bytes 786440 | tf_op jit(solution)/shard_map/ppermute | solution.py:15
  44.0 72.0 %copy-start.5 = (f32[1,128,128]{2,1,0:T(8,128)S(1)}, f32[1,128,128]{2,1,0:T(8,128)}, u32[]{:S(2)}) copy-start(f32[1,128,128]{2,1,0:T(8,128)} %param.8) | copy-start | bytes 196612
  45.9 323.3 %all-reduce.11.cloned.1.call-start = ((), (), s32[]{:S(2)}) async-start(), calls=%async_computation.1 | async-start | bytes 131072 | tf_op jit(solution)/shard_map/psum | solution.py:62
  125.8 10.9 %collective-permute-start.5 = (f32[512,128]{0,1:T(8,128)S(1)}, f32[512,128]{0,1:T(8,128)S(1)}, u32[]{:S(2)}, u32[]{:S(2)}) collective-permute-start(f32[512,128]{0,1:T(8,128)S(1)} %get-tuple-element.23), channel_id=1, source_target_pairs={{31,0},{0,1},{1,2},{2,3},{3,4},{4,5},{5,6},{6,7},{7,8},{8,9},{9,10... | collective-permute-start | bytes 786440 | tf_op jit(solution)/shard_map/ppermute | solution.py:15
  132.5 8.6 %collective-permute-start.6 = (f32[512,128]{0,1:T(8,128)}, f32[512,128]{0,1:T(8,128)S(1)}, u32[]{:S(2)}, u32[]{:S(2)}) collective-permute-start(f32[512,128]{0,1:T(8,128)} %get-tuple-element.22), channel_id=1, source_target_pairs={{1,0},{2,1},{3,2},{4,3},{5,4},{6,5},{7,6},{8,7},{9,8},{10,9},{11,1... | collective-permute-start | bytes 786440 | tf_op jit(solution)/shard_map/ppermute | solution.py:15
  132.6 11.6 %collective-permute-start.7 = (f32[512,128]{0,1:T(8,128)S(1)}, f32[512,128]{0,1:T(8,128)S(1)}, u32[]{:S(2)}, u32[]{:S(2)}) collective-permute-start(f32[512,128]{0,1:T(8,128)S(1)} %slice_select_fusion.2), channel_id=1, source_target_pairs={{2,0},{3,1},{4,2},{5,3},{6,4},{7,5},{8,6},{9,7},{10,8},{11,9},{12,... | collective-permute-start | bytes 786440 | tf_op jit(solution)/shard_map/ppermute | solution.py:15
  136.7 10.5 %collective-permute-start.4 = (f32[512,128]{0,1:T(8,128)}, f32[512,128]{0,1:T(8,128)}, u32[]{:S(2)}, u32[]{:S(2)}) collective-permute-start(f32[512,128]{0,1:T(8,128)} %get-tuple-element.21), channel_id=1, source_target_pairs={{30,0},{31,1},{0,2},{1,3},{2,4},{3,5},{4,6},{5,7},{6,8},{7,9},{8,1... | collective-permute-start | bytes 786440 | tf_op jit(solution)/shard_map/ppermute | solution.py:15
  305.5 317.1 %all-reduce.13.cloned.1.call-start = ((), (), s32[]{:S(2)}) async-start(), calls=%async_computation.2 | async-start | bytes 131072 | tf_op jit(solution)/shard_map/psum | solution.py:62
  374.1 11.2 %collective-permute-start.9 = (f32[512,128]{0,1:T(8,128)S(1)}, f32[512,128]{0,1:T(8,128)}, u32[]{:S(2)}, u32[]{:S(2)}) collective-permute-start(f32[512,128]{0,1:T(8,128)S(1)} %get-tuple-element.20), channel_id=1, source_target_pairs={{31,0},{0,1},{1,2},{2,3},{3,4},{4,5},{5,6},{6,7},{7,8},{8,9},{9,10... | collective-permute-start | bytes 786440 | tf_op jit(solution)/shard_map/ppermute | solution.py:15
  380.8 8.8 %collective-permute-start.10 = (f32[512,128]{0,1:T(8,128)}, f32[512,128]{0,1:T(8,128)}, u32[]{:S(2)}, u32[]{:S(2)}) collective-permute-start(f32[512,128]{0,1:T(8,128)} %get-tuple-element.19), channel_id=1, source_target_pairs={{1,0},{2,1},{3,2},{4,3},{5,4},{6,5},{7,6},{8,7},{9,8},{10,9},{11,1... | collective-permute-start | bytes 786440 | tf_op jit(solution)/shard_map/ppermute | solution.py:15
  381.5 11.1 %collective-permute-start.11 = (f32[512,128]{0,1:T(8,128)}, f32[512,128]{0,1:T(8,128)}, u32[]{:S(2)}, u32[]{:S(2)}) collective-permute-start(f32[512,128]{0,1:T(8,128)} %slice_select_fusion.1), channel_id=1, source_target_pairs={{2,0},{3,1},{4,2},{5,3},{6,4},{7,5},{8,6},{9,7},{10,8},{11,9},{12,... | collective-permute-start | bytes 786440 | tf_op jit(solution)/shard_map/ppermute | solution.py:15
  385.1 10.7 %collective-permute-start.8 = (f32[512,128]{0,1:T(8,128)}, f32[512,128]{0,1:T(8,128)}, u32[]{:S(2)}, u32[]{:S(2)}) collective-permute-start(f32[512,128]{0,1:T(8,128)} %get-tuple-element.18), channel_id=1, source_target_pairs={{30,0},{31,1},{0,2},{1,3},{2,4},{3,5},{4,6},{5,7},{6,8},{7,9},{8,1... | collective-permute-start | bytes 786440 | tf_op jit(solution)/shard_map/ppermute | solution.py:15
  627.4 11.3 %collective-permute-start.13 = (f32[512,128]{0,1:T(8,128)S(1)}, f32[512,128]{0,1:T(8,128)}, u32[]{:S(2)}, u32[]{:S(2)}) collective-permute-start(f32[512,128]{0,1:T(8,128)S(1)} %get-tuple-element.17), channel_id=1, source_target_pairs={{31,0},{0,1},{1,2},{2,3},{3,4},{4,5},{5,6},{6,7},{7,8},{8,9},{9,10... | collective-permute-start | bytes 786440 | tf_op jit(solution)/shard_map/ppermute | solution.py:15
  634.1 8.7 %collective-permute-start.14 = (f32[512,128]{0,1:T(8,128)}, f32[512,128]{0,1:T(8,128)}, u32[]{:S(2)}, u32[]{:S(2)}) collective-permute-start(f32[512,128]{0,1:T(8,128)} %get-tuple-element.16), channel_id=1, source_target_pairs={{1,0},{2,1},{3,2},{4,3},{5,4},{6,5},{7,6},{8,7},{9,8},{10,9},{11,1... | collective-permute-start | bytes 786440 | tf_op jit(solution)/shard_map/ppermute | solution.py:15
  634.9 11.1 %collective-permute-start.15 = (f32[512,128]{0,1:T(8,128)}, f32[512,128]{0,1:T(8,128)}, u32[]{:S(2)}, u32[]{:S(2)}) collective-permute-start(f32[512,128]{0,1:T(8,128)} %slice_select_fusion), channel_id=1, source_target_pairs={{2,0},{3,1},{4,2},{5,3},{6,4},{7,5},{8,6},{9,7},{10,8},{11,9},{12,... | collective-permute-start | bytes 786440 | tf_op jit(solution)/shard_map/ppermute | solution.py:15
  638.5 10.7 %collective-permute-start.12 = (f32[512,128]{0,1:T(8,128)}, f32[512,128]{0,1:T(8,128)}, u32[]{:S(2)}, u32[]{:S(2)}) collective-permute-start(f32[512,128]{0,1:T(8,128)} %get-tuple-element.15), channel_id=1, source_target_pairs={{30,0},{31,1},{0,2},{1,3},{2,4},{3,5},{4,6},{5,7},{6,8},{7,9},{8,1... | collective-permute-start | bytes 786440 | tf_op jit(solution)/shard_map/ppermute | solution.py:15
  649.1 83.0 %copy-start.16 = (f32[128]{0:T(128)S(1)}, f32[128]{0:T(128)}, u32[]{:S(2)}) copy-start(f32[128]{0:T(128)} %copy-done.15) | copy-start | bytes 1540
  649.1 83.0 %copy-start.18 = (f32[128]{0:T(128)S(1)}, f32[128]{0:T(128)}, u32[]{:S(2)}) copy-start(f32[128]{0:T(128)} %copy-done.17) | copy-start | bytes 1540
  (16 other events, 73.1 us)
Sparse Core Ops, SparseCore 0:
  46.1 69.9 all-reduce.8
  305.6 63.6 all-reduce.10
  558.8 63.7 all-reduce.12
where the time goes:
time: 756 us; the launch traced here: 746 us
  blocking collectives  381 us (50%)
  waiting for transfers between devices  187 us (25%)
  local copies, waits for them, and re-layouts  45.1 us (6%)
  starting transfers between devices  40.2 us (5%)
  matrix products  36 us (5%)
  other arithmetic  33.2 us (4%)
  between operations  23.7 us (3%)
    psum x3, blocking collectives, local(): lax.psum(jnp.sum(residual * residual, axis=0), ('cluster', 'sub'))  224 us
    psum x3, waiting for transfers between devices, local(): coarse_total = lax.psum(coarse_part, 'cluster')  183 us
    psum x2, blocking collectives, local(): curvature = lax.psum(jnp.sum(direction * image, axis=0), ('cluster', 'sub'))  157 us
    ppermute x16, starting transfers between devices, passed_along(): return lax.ppermute(block, axis, route)  40 us
    dynamic_update_slice x12, local copies, waits for them, and re-layouts, insert_run(): lax.dynamic_update_slice_in_dim(padded, run_block, start_row, 0)[:dual_rows]  22.4 us
    dot_general x3, matrix products, local(): jnp.dot(operator, direction.astype(jnp.bfloat16), preferred_element_type=...  20.7 us
  transfers between devices with their start and end apart: 19, of which 6 were waited for; matrix products, arithmetic and copies ran while one was open for 7% of the time, Pallas kernels for 0%

commit v1 on v0

--- a/solution.py
+++ b/solution.py
@@ -59,7 +59,11 @@
         )
         corner_values = jnp.dot(coupling, direction, precision=highest)
         coarse_part = jnp.dot(onehot.T, corner_values, precision=highest)
-        coarse_total = lax.psum(coarse_part, "cluster")
+        coarse_total = coarse_part
+        for hop in (1, 2, 4):
+            coarse_total = coarse_total + lax.ppermute(
+                coarse_total, "cluster", [(dev, dev ^ hop) for dev in range(8)]
+            )
         coarse_solution = jnp.dot(inverse, coarse_total, precision=highest)
         corner_back = jnp.dot(onehot, coarse_solution, precision=highest)
         image = assemble(local_part + jnp.dot(coupling.T, corner_back, precision=highest))

time: 756 us -> 586 us (0.78)
  waiting for transfers between devices: 187 us -> 23.5 us
  between operations: 23.7 us -> 11.2 us
  starting transfers between devices: 40.2 us -> 52 us
  matrix products: 36 us -> 27.2 us
    psum x3 -> x0, waiting for transfers between devices: 183 us -> none  [local(): coarse_total = lax.psum(coarse_part, 'cluster')]
    ppermute x0 -> x9, waiting for transfers between devices: none -> 19.3 us  [local(): lax.ppermute(coarse_total, 'cluster', [(dev, dev ^ hop) for dev in range(...]
    ppermute x0 -> x9, starting transfers between devices: none -> 17.1 us  [local(): lax.ppermute(coarse_total, 'cluster', [(dev, dev ^ hop) for dev in range(...]
  transfers between devices with their start and end apart: 19 -> 25, of which waited for: 6 -> 13; matrix products, arithmetic and copies ran while one was open for 7% -> 9% of each run, Pallas kernels for 0% -> 0%
where the time goes in v1:
time: 586 us; the launch traced here: 576 us
  blocking collectives  383 us (65%)
  starting transfers between devices  52 us (9%)
  local copies, waits for them, and re-layouts  45.1 us (8%)
  other arithmetic  33.4 us (6%)
  matrix products  27.2 us (5%)
  waiting for transfers between devices  23.5 us (4%)
  between operations  11.2 us (2%)
    psum x3, blocking collectives, local(): lax.psum(jnp.sum(residual * residual, axis=0), ('cluster', 'sub'))  228 us
    psum x2, blocking collectives, local(): curvature = lax.psum(jnp.sum(direction * image, axis=0), ('cluster', 'sub'))  156 us
    ppermute x16, starting transfers between devices, passed_along(): return lax.ppermute(block, axis, route)  34.8 us
    dynamic_update_slice x12, local copies, waits for them, and re-layouts, insert_run(): lax.dynamic_update_slice_in_dim(padded, run_block, start_row, 0)[:dual_rows]  22.3 us
    ppermute x9, waiting for transfers between devices, local(): lax.ppermute(coarse_total, 'cluster', [(dev, dev ^ hop) for dev in range(...  19.3 us
    dot_general x3, matrix products, local(): jnp.dot(operator, direction.astype(jnp.bfloat16), preferred_element_type=...  18.8 us
    ppermute x9, starting transfers between devices, local(): lax.ppermute(coarse_total, 'cluster', [(dev, dev ^ hop) for dev in range(...  17.1 us
    another operation x12, local copies, waits for them, and re-layouts  14.4 us
  transfers between devices with their start and end apart: 25, of which 13 were waited for; matrix products, arithmetic and copies ran while one was open for 9% of the time, Pallas kernels for 0%

profile of v1, /device:TPU:1, one launch (start us, length us, event | category | flops | bytes accessed | tf_op | source)
XLA Modules:
  0.0 575.8 jit_solution(4800720229232982307)
XLA Ops:
  16.4 4.8 collective-permute-start.3
  39.5 2.9 collective-permute-done.4
  44.2 3.0 collective-permute-done.5
  47.3 5.5 collective-permute-start.6
  56.7 6.3 %fusion.6 = f32[128,2048]{1,0:T(8,128)S(1)} fusion(f32[128,2048]{1,0:T(8,128)S(1)} %fusion.34, bf16[1,1,2048,2048]{3,2,1,0:T(8,128)(2,1)} %param.6, f32[2048,128]{0,1:T(8,128)S(1)} %fusion.12), kind=kOutput, calls=%fused_computation.8 | convolution fusion | flops 1074266112 | bytes 11534336 | tf_op jit(solution)/shard_map/dot_general | solution.py:57
  64.1 5.1 collective-permute-start.8
  69.7 5.0 collective-permute-start.10
  87.0 82.1 %all-reduce.4 = (f32[128]{0:T(128)S(1)}, f32[128]{0:T(128)S(1)}) all-reduce(f32[128]{0:T(128)} %get-tuple-element.5, f32[128]{0:T(128)} %get-tuple-element.4), channel_id=1, replica_groups=mesh['cluster'=8,'sub'=32] {'cluster','sub'}, use_global_device_ids=true, to_apply=%region_3.4 | all-reduce | flops 256 | bytes 2048 | tf_op jit(solution)/shard_map/psum | solution.py:55
  170.0 72.4 %psum.44 = f32[128]{0:T(128)S(1)} all-reduce(f32[128]{0:T(128)S(1)} %multiply_reduce_fusion.3), channel_id=1, replica_groups=mesh['cluster'=8,'sub'=32] {'cluster','sub'}, use_global_device_ids=true, to_apply=%region_7.8 | all-reduce | flops 128 | bytes 1024 | tf_op jit(solution)/shard_map/psum | solution.py:74
  249.1 3.9 collective-permute-done.12
  255.9 6.2 %fusion.2 = f32[128,2048]{1,0:T(8,128)S(1)} fusion(bf16[1,1,2048,2048]{3,2,1,0:T(8,128)(2,1)} %param.6, f32[2048,128]{0,1:T(8,128)S(1)} %multiply_add_fusion.1), kind=kOutput, calls=%fused_computation.2 | convolution fusion | flops 1074003968 | bytes 10485760 | tf_op jit(solution)/shard_map/dot_general | solution.py:57
  264.9 3.6 collective-permute-start.15
  269.3 4.5 collective-permute-start.17
  284.9 4.2 multiply_reduce_fusion.2
  289.1 77.5 %psum.45 = f32[128]{0:T(128)} all-reduce(f32[128]{0:T(128)} %get-tuple-element.12), channel_id=1, replica_groups=mesh['cluster'=8,'sub'=32] {'cluster','sub'}, use_global_device_ids=true, to_apply=%region_9.10 | all-reduce | flops 128 | bytes 1024 | tf_op jit(solution)/shard_map/psum | solution.py:70
  367.2 3.0 multiply_reduce_fusion.1
  370.2 73.1 %psum.46 = f32[128]{0:T(128)S(1)} all-reduce(f32[128]{0:T(128)} %get-tuple-element.10), channel_id=1, replica_groups=mesh['cluster'=8,'sub'=32] {'cluster','sub'}, use_global_device_ids=true, to_apply=%region_11.12 | all-reduce | flops 128 | bytes 1024 | tf_op jit(solution)/shard_map/psum | solution.py:74
  450.5 3.5 collective-permute-done.19
  456.8 6.2 %fusion = f32[128,2048]{1,0:T(8,128)S(1)} fusion(bf16[1,1,2048,2048]{3,2,1,0:T(8,128)(2,1)} %param.6, f32[2048,128]{0,1:T(8,128)S(1)} %multiply_add_fusion), kind=kOutput, calls=%fused_computation | convolution fusion | flops 1074003968 | bytes 10485760 | tf_op jit(solution)/shard_map/dot_general | solution.py:57
  465.8 3.5 collective-permute-start.22
  470.1 4.3 collective-permute-start.24
  485.5 3.7 multiply_reduce_fusion
  489.2 78.3 %psum.47 = f32[128]{0:T(128)} all-reduce(f32[128]{0:T(128)S(1)} %get-tuple-element.8), channel_id=1, replica_groups=mesh['cluster'=8,'sub'=32] {'cluster','sub'}, use_global_device_ids=true, to_apply=%region_13.14 | all-reduce | flops 128 | bytes 1024 | tf_op jit(solution)/shard_map/psum | solution.py:70
  568.2 3.3 subtract_bitcast_fusion
  (164 shorter events, 98.6 us)
Async XLA Ops:
  11.8 14.8 %collective-permute-start.1 = (f32[512,128]{0,1:T(8,128)S(1)}, f32[512,128]{0,1:T(8,128)S(1)}, u32[]{:S(2)}, u32[]{:S(2)}) collective-permute-start(f32[512,128]{0,1:T(8,128)S(1)} %bitcast_select_fusion.2), channel_id=1, source_target_pairs={{31,0},{0,1},{1,2},{2,3},{3,4},{4,5},{5,6},{6,7},{7,8},{8,9},{9,10... | collective-permute-start | bytes 786440 | tf_op jit(solution)/shard_map/ppermute | solution.py:15
  14.7 14.9 %collective-permute-start.2 = (f32[512,128]{0,1:T(8,128)S(1)}, f32[512,128]{0,1:T(8,128)}, u32[]{:S(2)}, u32[]{:S(2)}) collective-permute-start(f32[512,128]{0,1:T(8,128)S(1)} %bitcast_select_fusion.1), channel_id=1, source_target_pairs={{1,0},{2,1},{3,2},{4,3},{5,4},{6,5},{7,6},{8,7},{9,8},{10,9},{11,1... | collective-permute-start | bytes 786440 | tf_op jit(solution)/shard_map/ppermute | solution.py:15
  16.4 16.3 %collective-permute-start.3 = (f32[512,128]{0,1:T(8,128)S(1)}, f32[512,128]{0,1:T(8,128)S(1)}, u32[]{:S(2)}, u32[]{:S(2)}) collective-permute-start(f32[512,128]{0,1:T(8,128)S(1)} %fusion.38), channel_id=1, source_target_pairs={{2,0},{3,1},{4,2},{5,3},{6,4},{7,5},{8,6},{9,7},{10,8},{11,9},{12,... | collective-permute-start | bytes 786440 | tf_op jit(solution)/shard_map/ppermute | solution.py:15
  22.0 13.7 %collective-permute-start = (f32[512,128]{0,1:T(8,128)S(1)}, f32[512,128]{0,1:T(8,128)S(1)}, u32[]{:S(2)}, u32[]{:S(2)}) collective-permute-start(f32[512,128]{0,1:T(8,128)S(1)} %bitcast_select_fusion.3), channel_id=1, source_target_pairs={{30,0},{31,1},{0,2},{1,3},{2,4},{3,5},{4,6},{5,7},{6,8},{7,9},{8,1... | collective-permute-start | bytes 786440 | tf_op jit(solution)/shard_map/ppermute | solution.py:15
  39.2 3.2 collective-permute-start.4
  42.5 4.8 collective-permute-start.5
  47.3 7.9 %collective-permute-start.6 = (f32[128,128]{1,0:T(8,128)S(1)}, f32[128,128]{1,0:T(8,128)S(1)}, u32[]{:S(2)}, u32[]{:S(2)}) collective-permute-start(f32[128,128]{1,0:T(8,128)S(1)} %add.172), channel_id=1, source_target_pairs={{0,128},{32,160},{64,192},{96,224},{128,0},{160,32},{192,64},{224,... | collective-permute-start | bytes 196616 | tf_op jit(solution)/shard_map/ppermute | solution.py:64
  64.1 10.6 %collective-permute-start.8 = (f32[512,128]{0,1:T(8,128)S(1)}, f32[512,128]{0,1:T(8,128)S(1)}, u32[]{:S(2)}, u32[]{:S(2)}) collective-permute-start(f32[512,128]{0,1:T(8,128)S(1)} %get-tuple-element.23), channel_id=1, source_target_pairs={{31,0},{0,1},{1,2},{2,3},{3,4},{4,5},{5,6},{6,7},{7,8},{8,9},{9,10... | collective-permute-start | bytes 786440 | tf_op jit(solution)/shard_map/ppermute | solution.py:15
  69.2 8.9 %collective-permute-start.9 = (f32[512,128]{0,1:T(8,128)}, f32[512,128]{0,1:T(8,128)S(1)}, u32[]{:S(2)}, u32[]{:S(2)}) collective-permute-start(f32[512,128]{0,1:T(8,128)} %get-tuple-element.22), channel_id=1, source_target_pairs={{1,0},{2,1},{3,2},{4,3},{5,4},{6,5},{7,6},{8,7},{9,8},{10,9},{11,1... | collective-permute-start | bytes 786440 | tf_op jit(solution)/shard_map/ppermute | solution.py:15
  69.7 11.4 %collective-permute-start.10 = (f32[512,128]{0,1:T(8,128)S(1)}, f32[512,128]{0,1:T(8,128)S(1)}, u32[]{:S(2)}, u32[]{:S(2)}) collective-permute-start(f32[512,128]{0,1:T(8,128)S(1)} %slice_select_fusion.2), channel_id=1, source_target_pairs={{2,0},{3,1},{4,2},{5,3},{6,4},{7,5},{8,6},{9,7},{10,8},{11,9},{12,... | collective-permute-start | bytes 786440 | tf_op jit(solution)/shard_map/ppermute | solution.py:15
  74.7 9.6 %collective-permute-start.7 = (f32[512,128]{0,1:T(8,128)}, f32[512,128]{0,1:T(8,128)}, u32[]{:S(2)}, u32[]{:S(2)}) collective-permute-start(f32[512,128]{0,1:T(8,128)} %get-tuple-element.21), channel_id=1, source_target_pairs={{30,0},{31,1},{0,2},{1,3},{2,4},{3,5},{4,6},{5,7},{6,8},{7,9},{8,1... | collective-permute-start | bytes 786440 | tf_op jit(solution)/shard_map/ppermute | solution.py:15
  245.3 3.5 collective-permute-start.11
  248.8 4.1 collective-permute-start.12
  253.0 9.2 %collective-permute-start.13 = (f32[128,128]{1,0:T(8,128)S(1)}, f32[128,128]{1,0:T(8,128)S(1)}, u32[]{:S(2)}, u32[]{:S(2)}) collective-permute-start(f32[128,128]{1,0:T(8,128)S(1)} %add.182), channel_id=1, source_target_pairs={{0,128},{32,160},{64,192},{96,224},{128,0},{160,32},{192,64},{224,... | collective-permute-start | bytes 196616 | tf_op jit(solution)/shard_map/ppermute | solution.py:64
  264.9 8.9 %collective-permute-start.15 = (f32[512,128]{0,1:T(8,128)S(1)}, f32[512,128]{0,1:T(8,128)}, u32[]{:S(2)}, u32[]{:S(2)}) collective-permute-start(f32[512,128]{0,1:T(8,128)S(1)} %get-tuple-element.20), channel_id=1, source_target_pairs={{31,0},{0,1},{1,2},{2,3},{3,4},{4,5},{5,6},{6,7},{7,8},{8,9},{9,10... | collective-permute-start | bytes 786440 | tf_op jit(solution)/shard_map/ppermute | solution.py:15
  268.5 8.8 %collective-permute-start.16 = (f32[512,128]{0,1:T(8,128)}, f32[512,128]{0,1:T(8,128)}, u32[]{:S(2)}, u32[]{:S(2)}) collective-permute-start(f32[512,128]{0,1:T(8,128)} %get-tuple-element.19), channel_id=1, source_target_pairs={{1,0},{2,1},{3,2},{4,3},{5,4},{6,5},{7,6},{8,7},{9,8},{10,9},{11,1... | collective-permute-start | bytes 786440 | tf_op jit(solution)/shard_map/ppermute | solution.py:15
  269.3 11.1 %collective-permute-start.17 = (f32[512,128]{0,1:T(8,128)}, f32[512,128]{0,1:T(8,128)}, u32[]{:S(2)}, u32[]{:S(2)}) collective-permute-start(f32[512,128]{0,1:T(8,128)} %slice_select_fusion.1), channel_id=1, source_target_pairs={{2,0},{3,1},{4,2},{5,3},{6,4},{7,5},{8,6},{9,7},{10,8},{11,9},{12,... | collective-permute-start | bytes 786440 | tf_op jit(solution)/shard_map/ppermute | solution.py:15
  273.8 11.1 %collective-permute-start.14 = (f32[512,128]{0,1:T(8,128)}, f32[512,128]{0,1:T(8,128)}, u32[]{:S(2)}, u32[]{:S(2)}) collective-permute-start(f32[512,128]{0,1:T(8,128)} %get-tuple-element.18), channel_id=1, source_target_pairs={{30,0},{31,1},{0,2},{1,3},{2,4},{3,5},{4,6},{5,7},{6,8},{7,9},{8,1... | collective-permute-start | bytes 786440 | tf_op jit(solution)/shard_map/ppermute | solution.py:15
  449.9 4.1 collective-permute-start.19
  454.0 9.0 %collective-permute-start.20 = (f32[128,128]{1,0:T(8,128)S(1)}, f32[128,128]{1,0:T(8,128)S(1)}, u32[]{:S(2)}, u32[]{:S(2)}) collective-permute-start(f32[128,128]{1,0:T(8,128)S(1)} %add.193), channel_id=1, source_target_pairs={{0,128},{32,160},{64,192},{96,224},{128,0},{160,32},{192,64},{224,... | collective-permute-start | bytes 196616 | tf_op jit(solution)/shard_map/ppermute | solution.py:64
  465.8 8.6 %collective-permute-start.22 = (f32[512,128]{0,1:T(8,128)S(1)}, f32[512,128]{0,1:T(8,128)}, u32[]{:S(2)}, u32[]{:S(2)}) collective-permute-start(f32[512,128]{0,1:T(8,128)S(1)} %get-tuple-element.17), channel_id=1, source_target_pairs={{31,0},{0,1},{1,2},{2,3},{3,4},{4,5},{5,6},{6,7},{7,8},{8,9},{9,10... | collective-permute-start | bytes 786440 | tf_op jit(solution)/shard_map/ppermute | solution.py:15
  469.3 8.8 %collective-permute-start.23 = (f32[512,128]{0,1:T(8,128)}, f32[512,128]{0,1:T(8,128)}, u32[]{:S(2)}, u32[]{:S(2)}) collective-permute-start(f32[512,128]{0,1:T(8,128)} %get-tuple-element.16), channel_id=1, source_target_pairs={{1,0},{2,1},{3,2},{4,3},{5,4},{6,5},{7,6},{8,7},{9,8},{10,9},{11,1... | collective-permute-start | bytes 786440 | tf_op jit(solution)/shard_map/ppermute | solution.py:15
  470.1 11.1 %collective-permute-start.24 = (f32[512,128]{0,1:T(8,128)}, f32[512,128]{0,1:T(8,128)}, u32[]{:S(2)}, u32[]{:S(2)}) collective-permute-start(f32[512,128]{0,1:T(8,128)} %slice_select_fusion), channel_id=1, source_target_pairs={{2,0},{3,1},{4,2},{5,3},{6,4},{7,5},{8,6},{9,7},{10,8},{11,9},{12,... | collective-permute-start | bytes 786440 | tf_op jit(solution)/shard_map/ppermute | solution.py:15
  474.4 11.1 %collective-permute-start.21 = (f32[512,128]{0,1:T(8,128)}, f32[512,128]{0,1:T(8,128)}, u32[]{:S(2)}, u32[]{:S(2)}) collective-permute-start(f32[512,128]{0,1:T(8,128)} %get-tuple-element.15), channel_id=1, source_target_pairs={{30,0},{31,1},{0,2},{1,3},{2,4},{3,5},{4,6},{5,7},{6,8},{7,9},{8,1... | collective-permute-start | bytes 786440 | tf_op jit(solution)/shard_map/ppermute | solution.py:15
  (24 other events, 310.7 us)
